TPU v7x, 256 devices: a whole 4x4x8 slice. The times are simulated.
256 devices in a mesh: row: 8 (over y, x_hi), col: 32 (over z, x_lo, core).
Axes of the slice: x: 4 (x_hi: 2, x_lo: 2; x = x_hi * 2 + x_lo), y: 4, z: 8, core: 2. Of those that a mesh axis runs over, the one named last changes fastest.
Arguments:
- allele_doses: int32 [8192, 65536], P('row', 'col'), may hold values from 0 to 2
- disease_status: int32 [8192], P('row'), may hold values from 0 to 1
- walker_cloud: float32 [64, 65536], P(None, 'col'), may hold values from -21 to 21
- normal_perturbations: float32 [2, 64, 65536], P(None, None, 'col'), may hold values from -6 to 6
- approval_flags: int32 [2, 64], replicated, may hold values 0 or 1
- present_heat: float32 [1], replicated, may hold values from 0.85 to 0.92
- heat_advance: float32 [1], replicated, may hold values from 0.02 to 0.08
- drift_magnitude: float32 [1], replicated, may hold values from 0.8 to 1.2
Outputs:
- particles_out: float32 [64, 65536], P(None, 'col')
- log_weights: float32 [64], replicated
- mean_loglik: float32 [64], replicated
All inputs are finite; a program needn't handle non-finite values.
Results may differ from a plain program's by a relative error of at most 0.0035.
Values may be sent and summed in bfloat16 or wider, within the bound.
A program may use at most 64 MiB of HBM per device.

v0:
```python
import jax
import jax.numpy as jnp
from jax import lax
from jax.sharding import Mesh
from jax.sharding import PartitionSpec as P

P_SIZE = 65536
ROW = ("row_0", "row_1")
COL = ("col_0", "col_1", "col_2")
ROW_COL = ("row_0", "row_1", "col_0", "col_1", "col_2")


CLIP_FLOOR = 4.0
SHRINKAGE_LEVEL = 0.5


def in_blocks(shard, dim, count):
    before, after = (shard.shape[:dim], shard.shape[dim + 1 :])
    return jnp.moveaxis(shard.reshape(*before, count, -1, *after), dim, 0)


def summed_on_arrival(shard, axis, dim):
    count = lax.axis_size(axis)
    blocks = lax.all_to_all(in_blocks(shard, dim, count), axis, 0, 0, tiled=True)
    return jnp.sum(blocks, axis=0)


def one_axis_at_a_time(shard, axes):
    for axis in axes:
        shard = lax.psum(shard, axis)
    return shard


def copy_for_each(shard, axis):
    copies = jnp.broadcast_to(shard, (lax.axis_size(axis), *shard.shape))
    return lax.all_to_all(copies, axis, split_axis=0, concat_axis=0, tiled=True)


def joined_along(blocks, dim):
    dims = list(blocks.shape[1:])
    dims[dim] *= blocks.shape[0]
    return jnp.moveaxis(blocks, 0, dim).reshape(dims)


def collect(shard, axis, dim):
    blocks = copy_for_each(shard, axis)
    return joined_along(blocks, dim)


def of_everyone(shard, axis):
    return copy_for_each(shard, axis).astype(jnp.float32).sum(axis=0)


def of_everyone_2(shard, axis):
    everything = copy_for_each(shard, axis)
    return jnp.sum(everything, axis=0)


def contract_cols(left, right):
    return lax.dot_general(
        left, right, (((1,), (1,)), ((), ())), preferred_element_type=jnp.float32
    )


def contract_rows(left, right):
    return lax.dot_general(
        left, right, (((0,), (0,)), ((), ())), preferred_element_type=jnp.float32
    )


def local(
    allele_doses,
    disease_status,
    walker_cloud,
    normal_perturbations,
    approval_flags,
    present_heat,
    heat_advance,
    drift_magnitude,
):
    reciprocal_square = float(P_SIZE) ** (-0.5)
    centered = (allele_doses - 1).astype(jnp.bfloat16)
    outcome_all = disease_status.astype(jnp.float32)
    local_rows = centered.shape[0]
    total_rows = local_rows * lax.axis_size(ROW)
    share = local_rows // lax.axis_size(COL)
    upcoming_heat = present_heat[0] + heat_advance[0]
    stepped = drift_magnitude[0]
    outcome = lax.dynamic_slice_in_dim(outcome_all, lax.axis_index(COL) * share, share, 0)

    def logits_of(regression_weight):
        coef_bf = regression_weight.astype(jnp.bfloat16)
        return summed_on_arrival(contract_cols(centered, coef_bf), COL, 0) * reciprocal_square

    def loglik_of(linear_predictor):
        shard_partial_total = jnp.sum(
            outcome[:, None] * linear_predictor - jax.nn.softplus(linear_predictor), axis=0
        )
        return one_axis_at_a_time(shard_partial_total, ROW_COL)

    linear_predictor = logits_of(walker_cloud)
    loglik = loglik_of(linear_predictor)
    scaled = heat_advance[0] * loglik
    clipped = jnp.maximum(scaled - jnp.max(scaled), -CLIP_FLOOR)
    log_weights = clipped - jnp.log(jnp.sum(jnp.exp(clipped)))
    weights = jnp.exp(log_weights)
    center = jnp.sum(weights[:, None] * walker_cloud, axis=0)
    spread = jnp.sum(weights[:, None] * (walker_cloud - center[None, :]) ** 2, axis=0) + 1e-06
    spread_total = of_everyone_2(jnp.sum(spread), COL)
    precond = spread / (spread_total / P_SIZE)
    regression_weight = walker_cloud
    for move in range(2):
        residual_bf = (outcome[:, None] - jax.nn.sigmoid(linear_predictor)).astype(jnp.bfloat16)
        partial_sum = contract_rows(collect(residual_bf, COL, 0), centered)
        fitness_slope = of_everyone(partial_sum.astype(jnp.bfloat16), ROW).astype(jnp.float32)
        slope_vector = (
            upcoming_heat * reciprocal_square * fitness_slope
            - SHRINKAGE_LEVEL
            * regression_weight
            / jnp.sqrt(regression_weight * regression_weight + 1.0)
        )
        proposal = (
            regression_weight
            + stepped * precond[None, :] * slope_vector
            + jnp.sqrt(2.0 * stepped * precond)[None, :] * normal_perturbations[move]
        )
        regression_weight = jnp.where(
            approval_flags[move][:, None] == 1, proposal, regression_weight
        )
        linear_predictor = logits_of(regression_weight)
    mean_loglik = loglik_of(linear_predictor) / total_rows
    return (regression_weight, log_weights, mean_loglik)


def solution(mesh):
    torus = Mesh(mesh.devices.reshape(4, 2, 8, 2, 2), ("row_0", "row_1", "col_0", "col_1", "col_2"))
    return jax.shard_map(
        local,
        mesh=torus,
        in_specs=(P(ROW, COL), P(ROW), P(None, COL), P(None, None, COL), P(), P(), P(), P()),
        out_specs=(P(None, COL), P(), P()),
        check_vma=False,
    )
```

profile of v0, /device:TPU:1, one launch (start us, length us, event | category | flops | bytes accessed | tf_op | source)
XLA Modules:
  0.0 265.9 jit_solution(11727277135658643191)
XLA Ops:
  0.6 4.6 %add_convert_fusion = bf16[1024,2048]{1,0:T(8,128)(2,1)S(1)} fusion(s32[1024,2048]{1,0:T(8,128)} %param.8), kind=kLoop, calls=%fused_computation | loop fusion | flops 4194304 | bytes 12582912 | tf_op jit(solution)/shard_map/convert_element_type | solution.py:82
  5.3 1.9 copy-done
  7.2 1.2 fusion.8
  8.4 1.0 reshape.59
  9.5 11.0 %all-to-all-start = ((f32[32,1,2048]{2,1,0:T(1,128)}), f32[32,1,2048]{2,1,0:T(1,128)S(1)}, u32[]{:S(2)}, u32[]{:S(2)}) async-start(f32[32,1,2048]{2,1,0:T(1,128)} %reshape.59), calls=%async_computation | async-start | bytes 524288 | tf_op jit(solution)/shard_map/all_to_all | solution.py:24
  21.2 0.1 broadcast_multiply_fusion.2
  21.3 10.7 %all-to-all-done = f32[32,1,2048]{2,1,0:T(1,128)S(1)} async-done(((f32[32,1,2048]{2,1,0:T(1,128)}), f32[32,1,2048]{2,1,0:T(1,128)S(1)}, u32[]{:S(2)}, u32[]{:S(2)}) %all-to-all-start) | async-done | bytes 262176 | tf_op jit(solution)/shard_map/all_to_all | solution.py:24
  31.9 0.5 broadcast.82
  32.5 1.3 reduce.1
  33.7 0.2 reshape.60
  33.9 0.1 reduce_sum.108
  34.0 0.1 fusion.11
  34.1 8.7 %psum.70 = f32[64]{0:T(128)S(1)} all-reduce(f32[64]{0:T(128)S(1)} %get-tuple-element.7), channel_id=1, replica_groups=mesh['row_0'=4,'row_1'=2,'col_0'=8,'col_1'=2,'col_2'=2] {'row_0'}, use_global_device_ids=true, to_apply=%region_2.3 | all-reduce | flops 64 | bytes 512 | tf_op jit(solution)/shard_map/psum | solution.py:30
  42.8 5.3 %psum.71 = f32[64]{0:T(128)S(1)} all-reduce(f32[64]{0:T(128)S(1)} %psum.70), channel_id=1, replica_groups=mesh['row_0'=4,'row_1'=2,'col_0'=8,'col_1'=2,'col_2'=2] {'row_1'}, use_global_device_ids=true, to_apply=%region_3.4 | all-reduce | flops 64 | bytes 512 | tf_op jit(solution)/shard_map/psum | solution.py:30
  48.1 11.7 %psum.72 = f32[64]{0:T(128)S(1)} all-reduce(f32[64]{0:T(128)S(1)} %psum.71), channel_id=1, replica_groups=mesh['row_0'=4,'row_1'=2,'col_0'=8,'col_1'=2,'col_2'=2] {'col_0'}, use_global_device_ids=true, to_apply=%region_4.5 | all-reduce | flops 64 | bytes 512 | tf_op jit(solution)/shard_map/psum | solution.py:30
  59.8 3.8 %psum.73 = f32[64]{0:T(128)S(1)} all-reduce(f32[64]{0:T(128)S(1)} %psum.72), channel_id=1, replica_groups=mesh['row_0'=4,'row_1'=2,'col_0'=8,'col_1'=2,'col_2'=2] {'col_1'}, use_global_device_ids=true, to_apply=%region_5.6 | all-reduce | flops 64 | bytes 512 | tf_op jit(solution)/shard_map/psum | solution.py:30
  63.5 10.9 %psum.74 = f32[64]{0:T(128)S(1)} all-reduce(f32[64]{0:T(128)S(1)} %psum.73), channel_id=1, replica_groups=mesh['row_0'=4,'row_1'=2,'col_0'=8,'col_1'=2,'col_2'=2] {'col_2'}, use_global_device_ids=true, to_apply=%region_6.7 | all-reduce | flops 64 | bytes 512 | tf_op jit(solution)/shard_map/psum | solution.py:30
  74.4 0.6 multiply_reduce_fusion.2
  75.1 1.2 exponential_reduce_fusion
  77.0 0.8 reshape.61
  77.9 4.9 %all-to-all-start.2 = ((bf16[32,2,1024]{2,1,0:T(2,128)(2,1)}), bf16[32,2,1024]{2,1,0:T(2,128)(2,1)S(1)}, u32[]{:S(2)}, u32[]{:S(2)}) async-start(bf16[32,2,1024]{2,1,0:T(2,128)(2,1)} %reshape.61), calls=%async_computation.2 | async-start | bytes 262144 | tf_op jit(solution)/shard_map/all_to_all | solution.py:36
  82.8 1.1 fusion.14
  83.9 0.1 multiply_reduce_fusion.1
  84.0 0.2 multiply_reduce_fusion
  84.2 0.6 add_reduce_fusion
  84.8 7.2 %all-to-all-done.2 = bf16[32,2,1024]{2,1,0:T(2,128)(2,1)S(1)} async-done(((bf16[32,2,1024]{2,1,0:T(2,128)(2,1)}), bf16[32,2,1024]{2,1,0:T(2,128)(2,1)S(1)}, u32[]{:S(2)}, u32[]{:S(2)}) %all-to-all-start.2) | async-done | bytes 131104 | tf_op jit(solution)/shard_map/all_to_all | solution.py:36
  92.0 1.2 broadcast_in_dim.41
  93.2 3.9 %all-to-all-start.1 = ((f32[32,1,1]{2,1,0:T(1,128)}), f32[32,1,1]{2,1,0:T(1,128)S(1)}, u32[]{:S(2)}, u32[]{:S(2)}) async-start(f32[32,1,1]{2,1,0:T(1,128)} %broadcast_in_dim.41), calls=%async_computation.1 | async-start | bytes 32768 | tf_op jit(solution)/shard_map/all_to_all | solution.py:36
  97.2 0.2 reshape.62
  97.4 3.1 %convolution_convert_fusion.1 = bf16[64,2048]{1,0:T(8,128)(2,1)S(1)} fusion(bf16[1024,64]{1,0:T(8,128)(2,1)S(1)} %bitcast.41, bf16[1024,2048]{1,0:T(8,128)(2,1)} %copy-done), kind=kOutput, calls=%fused_computation.4 | convolution fusion | flops 268566528 | bytes 4587520 | tf_op jit(solution)/shard_map/dot_general | solution.py:66
  100.5 4.6 %all-to-all-done.1 = f32[32,1,1]{2,1,0:T(1,128)S(1)} async-done(((f32[32,1,1]{2,1,0:T(1,128)}), f32[32,1,1]{2,1,0:T(1,128)S(1)}, u32[]{:S(2)}, u32[]{:S(2)}) %all-to-all-start.1) | async-done | bytes 160 | tf_op jit(solution)/shard_map/all_to_all | solution.py:36
  105.1 1.6 broadcast_in_dim.43
  106.7 4.0 %all-to-all-start.3 = ((bf16[8,64,2048]{2,1,0:T(8,128)(2,1)}), bf16[8,64,2048]{2,1,0:T(8,128)(2,1)S(1)}, u32[]{:S(2)}, u32[]{:S(2)}) async-start(bf16[8,64,2048]{2,1,0:T(8,128)(2,1)} %broadcast_in_dim.43), calls=%async_computation.3 | async-start | bytes 4194304 | tf_op jit(solution)/shard_map/all_to_all | solution.py:36
  112.1 0.6 reduce_sum.114
  113.3 25.1 %all-to-all-done.3 = bf16[8,64,2048]{2,1,0:T(8,128)(2,1)S(1)} async-done(((bf16[8,64,2048]{2,1,0:T(8,128)(2,1)}), bf16[8,64,2048]{2,1,0:T(8,128)(2,1)S(1)}, u32[]{:S(2)}, u32[]{:S(2)}) %all-to-all-start.3) | async-done | bytes 2097184 | tf_op jit(solution)/shard_map/all_to_all | solution.py:36
  138.4 0.3 convert_reduce_fusion.1
  138.8 1.5 fusion.3
  140.2 0.5 copy-done.1
  140.8 1.2 fusion.6
  142.0 0.3 reshape.63
  142.3 15.9 %all_to_all.41 = f32[32,1,2048]{2,1,0:T(1,128)S(1)} all-to-all(f32[32,1,2048]{2,1,0:T(1,128)S(1)} %reshape.63), channel_id=1, replica_groups=mesh['row_0'=4,'row_1'=2,'col_0'=8,'col_1'=2,'col_2'=2] {'col_0','col_1'..., dimensions={0} | all-to-all | bytes 524288 | tf_op jit(solution)/shard_map/all_to_all | solution.py:24
  158.2 1.3 reduce.2
  159.5 0.2 reshape.64
  159.8 0.1 subtract_convert_fusion
  159.9 0.2 reshape.65
  160.1 13.2 %all_to_all.42 = bf16[32,2,1024]{2,1,0:T(2,128)(2,1)S(1)} all-to-all(bf16[32,2,1024]{2,1,0:T(2,128)(2,1)S(1)} %reshape.65), channel_id=1, replica_groups=mesh['row_0'=4,'row_1'=2,'col_0'=8,'col_1'=2,'col_2'=2] {'col_0','col_1'..., dimensions={0} | all-to-all | bytes 262144 | tf_op jit(solution)/shard_map/all_to_all | solution.py:36
  173.3 0.2 reshape.66
  173.5 3.1 %convolution_convert_fusion = bf16[64,2048]{1,0:T(8,128)(2,1)S(1)} fusion(bf16[1024,64]{1,0:T(8,128)(2,1)S(1)} %bitcast.42, bf16[1024,2048]{1,0:T(8,128)(2,1)} %copy-done), kind=kOutput, calls=%fused_computation.3 | convolution fusion | flops 268566528 | bytes 4587520 | tf_op jit(solution)/shard_map/dot_general | solution.py:66
  176.6 0.2 broadcast_in_dim.45
  176.8 30.5 %all_to_all.43 = bf16[8,64,2048]{2,1,0:T(8,128)(2,1)S(1)} all-to-all(bf16[8,64,2048]{2,1,0:T(8,128)(2,1)S(1)} %broadcast_in_dim.45), channel_id=1, replica_groups=mesh['row_0'=4,'row_1'=2,'col_0'=8,'col_1'=2,'col_2'=2] {'row_0','row_1'}, dimensions={0} | all-to-all | bytes 4194304 | tf_op jit(solution)/shard_map/all_to_all | solution.py:36
  207.3 0.4 convert_reduce_fusion
  207.7 0.2 fusion.1
  208.0 1.2 fusion.4
  209.2 0.3 reshape.67
  209.6 16.0 %all_to_all.44 = f32[32,1,2048]{2,1,0:T(1,128)S(1)} all-to-all(f32[32,1,2048]{2,1,0:T(1,128)S(1)} %reshape.67), channel_id=1, replica_groups=mesh['row_0'=4,'row_1'=2,'col_0'=8,'col_1'=2,'col_2'=2] {'col_0','col_1'..., dimensions={0} | all-to-all | bytes 524288 | tf_op jit(solution)/shard_map/all_to_all | solution.py:24
  225.6 1.3 reduce.3
  226.8 0.2 reshape.68
  227.1 0.1 fusion.13
  227.2 6.6 %psum.75 = f32[64]{0:T(128)S(1)} all-reduce(f32[64]{0:T(128)S(1)} %fusion.13), channel_id=1, replica_groups=mesh['row_0'=4,'row_1'=2,'col_0'=8,'col_1'=2,'col_2'=2] {'row_0'}, use_global_device_ids=true, to_apply=%region_18.19 | all-reduce | flops 64 | bytes 512 | tf_op jit(solution)/shard_map/psum | solution.py:30
  233.8 5.3 %psum.76 = f32[64]{0:T(128)S(1)} all-reduce(f32[64]{0:T(128)S(1)} %psum.75), channel_id=1, replica_groups=mesh['row_0'=4,'row_1'=2,'col_0'=8,'col_1'=2,'col_2'=2] {'row_1'}, use_global_device_ids=true, to_apply=%region_19.20 | all-reduce | flops 64 | bytes 512 | tf_op jit(solution)/shard_map/psum | solution.py:30
  239.0 11.7 %psum.77 = f32[64]{0:T(128)S(1)} all-reduce(f32[64]{0:T(128)S(1)} %psum.76), channel_id=1, replica_groups=mesh['row_0'=4,'row_1'=2,'col_0'=8,'col_1'=2,'col_2'=2] {'col_0'}, use_global_device_ids=true, to_apply=%region_20.21 | all-reduce | flops 64 | bytes 512 | tf_op jit(solution)/shard_map/psum | solution.py:30
  250.7 3.8 %psum.78 = f32[64]{0:T(128)S(1)} all-reduce(f32[64]{0:T(128)S(1)} %psum.77), channel_id=1, replica_groups=mesh['row_0'=4,'row_1'=2,'col_0'=8,'col_1'=2,'col_2'=2] {'col_1'}, use_global_device_ids=true, to_apply=%region_21.22 | all-reduce | flops 64 | bytes 512 | tf_op jit(solution)/shard_map/psum | solution.py:30
  254.5 10.9 %psum.79 = f32[64]{0:T(128)S(1)} all-reduce(f32[64]{0:T(128)S(1)} %psum.78), channel_id=1, replica_groups=mesh['row_0'=4,'row_1'=2,'col_0'=8,'col_1'=2,'col_2'=2] {'col_2'}, use_global_device_ids=true, to_apply=%region_22.23 | all-reduce | flops 64 | bytes 512 | tf_op jit(solution)/shard_map/psum | solution.py:30
  265.4 0.5 broadcast_multiply_fusion.1
  (21 shorter events, 0.2 us)
Async XLA Ops:
  0.6 6.6 %copy-start.3 = (f32[64,2048]{1,0:T(8,128)S(1)}, f32[64,2048]{1,0:T(8,128)}, u32[]{:S(2)}) copy-start(f32[64,2048]{1,0:T(8,128)} %param.10) | copy-start | bytes 1572868
  5.3 1.9 copy-start
  7.2 14.0 %copy-start.6 = (s32[1024]{0:T(1024)S(1)}, s32[1024]{0:T(1024)}, u32[]{:S(2)}) copy-start(s32[1024]{0:T(1024)} %param.9) | copy-start | bytes 12292
  9.5 22.5 %all-to-all-start = ((f32[32,1,2048]{2,1,0:T(1,128)}), f32[32,1,2048]{2,1,0:T(1,128)S(1)}, u32[]{:S(2)}, u32[]{:S(2)}) async-start(f32[32,1,2048]{2,1,0:T(1,128)} %reshape.59), calls=%async_computation | async-start | bytes 524288 | tf_op jit(solution)/shard_map/all_to_all | solution.py:24
  77.9 14.1 %all-to-all-start.2 = ((bf16[32,2,1024]{2,1,0:T(2,128)(2,1)}), bf16[32,2,1024]{2,1,0:T(2,128)(2,1)S(1)}, u32[]{:S(2)}, u32[]{:S(2)}) async-start(bf16[32,2,1024]{2,1,0:T(2,128)(2,1)} %reshape.61), calls=%async_computation.2 | async-start | bytes 262144 | tf_op jit(solution)/shard_map/all_to_all | solution.py:36
  93.2 11.9 %all-to-all-start.1 = ((f32[32,1,1]{2,1,0:T(1,128)}), f32[32,1,1]{2,1,0:T(1,128)S(1)}, u32[]{:S(2)}, u32[]{:S(2)}) async-start(f32[32,1,1]{2,1,0:T(1,128)} %broadcast_in_dim.41), calls=%async_computation.1 | async-start | bytes 32768 | tf_op jit(solution)/shard_map/all_to_all | solution.py:36
  100.5 11.6 %copy-start.7 = (s32[2,64]{1,0:T(2,128)S(1)}, s32[2,64]{1,0:T(2,128)}, u32[]{:S(2)}) copy-start(s32[2,64]{1,0:T(2,128)} %param.12) | copy-start | bytes 1540
  106.7 31.7 %all-to-all-start.3 = ((bf16[8,64,2048]{2,1,0:T(8,128)(2,1)}), bf16[8,64,2048]{2,1,0:T(8,128)(2,1)S(1)}, u32[]{:S(2)}, u32[]{:S(2)}) async-start(bf16[8,64,2048]{2,1,0:T(8,128)(2,1)} %broadcast_in_dim.43), calls=%async_computation.3 | async-start | bytes 4194304 | tf_op jit(solution)/shard_map/all_to_all | solution.py:36
  138.4 2.3 copy-start.1
  176.6 31.1 %copy-start.5 = (f32[2,64,2048]{2,1,0:T(8,128)S(1)}, f32[2,64,2048]{2,1,0:T(8,128)}, u32[]{:S(2)}) copy-start(f32[2,64,2048]{2,1,0:T(8,128)} %param.11) | copy-start | bytes 3145732
  176.8 31.1 %copy-start.2 = (bf16[1024,2048]{1,0:T(8,128)(2,1)S(1)}, bf16[1024,2048]{1,0:T(8,128)(2,1)}, u32[]{:S(2)}) copy-start(bf16[1024,2048]{1,0:T(8,128)(2,1)} %copy-done) | copy-start | bytes 12582916
  208.0 19.1 %copy-start.4 = (f32[64,2048]{1,0:T(8,128)}, f32[64,2048]{1,0:T(8,128)S(1)}, u32[]{:S(2)}) copy-start(f32[64,2048]{1,0:T(8,128)S(1)} %fusion.1) | copy-start | bytes 1572868
where the time goes:
time: 267 us; the launch traced here: 266 us
  blocking collectives  154 us (58%)
  waiting for transfers between devices  47.6 us (18%)
  starting transfers between devices  23.9 us (9%)
  other arithmetic  16.3 us (6%)
  local copies, waits for them, and re-layouts  9.93 us (4%)
  matrix products  9.84 us (4%)
  between operations  4.21 us (2%)
    psum x10, blocking collectives, one_axis_at_a_time(): shard = lax.psum(shard, axis)  78.5 us
    all_to_all x2, blocking collectives, copy_for_each(): return lax.all_to_all(copies, axis, split_axis=0, concat_axis=0, tiled=True)  43.7 us
    all_to_all x3, waiting for transfers between devices, copy_for_each(): return lax.all_to_all(copies, axis, split_axis=0, concat_axis=0, tiled=True)  36.9 us
    all_to_all x2, blocking collectives, summed_on_arrival(): lax.all_to_all(in_blocks(shard, dim, count), axis, 0, 0, tiled=True)  31.9 us
    all_to_all x3, starting transfers between devices, copy_for_each(): return lax.all_to_all(copies, axis, split_axis=0, concat_axis=0, tiled=True)  12.9 us
    all_to_all x1, starting transfers between devices, summed_on_arrival(): lax.all_to_all(in_blocks(shard, dim, count), axis, 0, 0, tiled=True)  11 us
    all_to_all x1, waiting for transfers between devices, summed_on_arrival(): lax.all_to_all(in_blocks(shard, dim, count), axis, 0, 0, tiled=True)  10.7 us
    unnamed x26, local copies, waits for them, and re-layouts  6.28 us
  transfers between devices with their start and end apart: 4, of which 4 were waited for; matrix products, arithmetic and copies ran while one was open for 2% of the time, Pallas kernels for 0%

commit v1 on v0

v1 whole, which is shorter than its diff:
```python
import jax
import jax.numpy as jnp
from jax import lax
from jax.experimental import pallas as pl
from jax.experimental.pallas import tpu as pltpu
from jax.sharding import Mesh
from jax.sharding import PartitionSpec as P

P_SIZE = 65536
K = 64
ROW = ("row_0", "row_1")
COL = ("col_0", "col_1", "col_2")
CLIP_FLOOR = 4.0
SHRINKAGE_LEVEL = 0.5
MESH = pl.DeviceIdType.MESH

ROWS = 1024
COLS = 2048
NZ, NQ, NT, NR = 8, 4, 32, 8
TP = 128
TK = 16
WR = COLS // NR
NMOVE = 2
ROW_OFFSETS = ((2, 1), (1, 1), (3, 1), (2, 0), (0, 1), (1, 0), (3, 0))


def kernel(
    x_hbm, y_ref, c_hbm, noise_hbm, flags_ref, heat_ref, adv_ref, drift_ref,
    out_hbm, lw_ref, ml_ref,
    xi, xb, c, noise, cb, base, spread, scale, rfull,
    pf, rf, ps, rs, resid, gsend, grecv, hfull,
    ll_send, ll_col, llr_send, llr, sp_send, sp_col,
    xsem, lsem, osem, ssem, rsem,
):
    f32, bf16 = jnp.float32, jnp.bfloat16
    y, xh = lax.axis_index("row_0"), lax.axis_index("row_1")
    z, xl, co = lax.axis_index("col_0"), lax.axis_index("col_1"), lax.axis_index("col_2")
    q = xl * 2 + co
    me = z * NQ + q
    rho = y * 2 + xh
    scale_s = float(P_SIZE) ** (-0.5)

    def z_at(k):
        off = 4 + (1 - 2 * lax.rem(k, 2)) * ((k + 1) // 2)
        return lax.rem(z + off, NZ)

    copy_c = pltpu.make_async_copy(c_hbm, c, lsem.at[0])
    copy_c.start()

    def x_copy(k):
        rows = pl.ds(pl.multiple_of(z_at(k) * TP, TP), TP)
        return pltpu.make_async_copy(x_hbm.at[rows], xi.at[k], xsem.at[k])

    @pl.loop(0, NZ)
    def _(k):
        x_copy(k).start()

    copy_noise = pltpu.make_async_copy(noise_hbm, noise, lsem.at[1])
    copy_noise.start()

    barrier = pltpu.get_barrier_semaphore()

    def col_id(d):
        return (y, xh, d // NQ, lax.rem(d // 2, 2), lax.rem(d, 2))

    def row_id(o):
        return (lax.rem(y + o[0], 4), lax.rem(xh + o[1], 2), z, xl, co)

    @pl.loop(1, NT)
    def _(r):
        pl.semaphore_signal(barrier, inc=1, device_id=col_id(lax.rem(me + r, NT)), device_id_type=MESH)

    for o in ROW_OFFSETS:
        pl.semaphore_signal(barrier, inc=1, device_id=row_id(o), device_id_type=MESH)

    def landed(ref, sem):
        pltpu.make_async_copy(ref, ref, sem).wait()

    def to_col(src, dst, sems, send_at, recv_at):
        @pl.loop(0, NZ)
        def _(k):
            zd = z_at(k)
            for qd in range(NQ):
                @pl.when(jnp.logical_or(zd != z, qd != q))
                def _():
                    pltpu.make_async_remote_copy(
                        src_ref=src, dst_ref=dst, send_sem=send_at, recv_sem=recv_at,
                        device_id=(y, xh, zd, qd // 2, qd % 2), device_id_type=MESH,
                    ).start()

    def to_row(src, dst, send_at, recv_at):
        for o in ROW_OFFSETS:
            pltpu.make_async_remote_copy(
                src_ref=src, dst_ref=dst, send_sem=send_at, recv_sem=recv_at,
                device_id=row_id(o), device_id_type=MESH,
            ).start()

    def logits_phase(t, sent, got, n):
        @pl.loop(0, NZ)
        def _(k):
            zd = z_at(k)
            rows = pl.ds(pl.multiple_of(zd * TP, TP), TP)
            if t == 0:
                x_copy(k).wait()
                xb[rows, :] = (xi[k].astype(f32) - 1.0).astype(bf16)
            part = lax.dot_general(
                cb[...], xb[rows, :], (((1,), (1,)), ((), ())), preferred_element_type=f32
            )
            for qd in range(NQ):
                sent[zd * NQ + qd] = part[qd * TK:(qd + 1) * TK, :].astype(sent.dtype)
            for qd in range(NQ):
                @pl.when(jnp.logical_or(zd != z, qd != q))
                def _():
                    pltpu.make_async_remote_copy(
                        src_ref=sent.at[zd * NQ + qd], dst_ref=got.at[me],
                        send_sem=ssem.at[n], recv_sem=rsem.at[n],
                        device_id=(y, xh, zd, qd // 2, qd % 2), device_id_type=MESH,
                    ).start()
        got[me] = sent[me]
        landed(got.at[pl.ds(0, NT - 1)], rsem.at[n])
        return jnp.sum(got[...].astype(f32), axis=0) * scale_s

    outcome = y_ref[pl.ds(z, 1), :].astype(f32)
    sub = lax.broadcasted_iota(jnp.int32, (TK, TP), 0)
    lane = lax.broadcasted_iota(jnp.int32, (TK, TP), 1)

    def loglik_row(tile):
        soft = jnp.maximum(tile, 0.0) + jnp.log1p(jnp.exp(-jnp.abs(tile)))
        total = jnp.sum(outcome * tile - soft, axis=1, keepdims=True)
        return jnp.sum(jnp.where(lane == sub + q * TK, total, 0.0), axis=0, keepdims=True)

    eye = lax.broadcasted_iota(jnp.int32, (K, TP), 0) == lax.broadcasted_iota(jnp.int32, (K, TP), 1)

    def as_column(row):
        return jnp.sum(jnp.where(eye, row, 0.0), axis=1, keepdims=True)

    flags = [
        as_column(flags_ref[t:t + 1, :].astype(f32)) > 0.5 for t in range(NMOVE)
    ]
    present = heat_ref[0]
    advance = adv_ref[0]
    stepped = drift_ref[0]
    upcoming = present + advance

    copy_c.wait()
    cb[...] = c[...].astype(bf16)
    pl.semaphore_wait(barrier, NT - 1 + NR - 1)
    tile = logits_phase(0, pf, rf, 0)

    def loglik_send(u, tile):
        ll_send[u] = loglik_row(tile)
        ll_col[u, me] = ll_send[u]
        to_col(ll_send.at[u], ll_col.at[u, me], None, ssem.at[10 + u], rsem.at[10 + u])

    def loglik_over_col(u):
        landed(ll_col.at[u, pl.ds(0, NT - 1)], rsem.at[10 + u])
        llr_send[u] = jnp.sum(ll_col[u], axis=0)
        llr[u, rho] = llr_send[u]
        to_row(llr_send.at[u], llr.at[u, rho], ssem.at[12 + u], rsem.at[12 + u])

    def loglik_total(u):
        landed(llr.at[u, pl.ds(0, NR - 1)], rsem.at[12 + u])
        return jnp.sum(llr[u], axis=0)

    copy_noise.wait()
    for t in range(NMOVE):
        resid[t, me] = (outcome - jax.nn.sigmoid(tile)).astype(bf16)
        to_col(resid.at[t, me], resid.at[t, me], None, ssem.at[3 + t], rsem.at[3 + t])
        if t == 0:
            loglik_send(0, tile)
        landed(resid.at[t, pl.ds(0, NT - 1)], rsem.at[3 + t])
        for p in range(NZ):
            rfull[:, p * TP:(p + 1) * TP] = resid[t, p * NQ:(p + 1) * NQ].reshape(K, TP)

        def share(d):
            cols = pl.ds(pl.multiple_of(d * WR, WR), WR)
            return jnp.dot(rfull[...], xb[:, cols], preferred_element_type=f32).astype(bf16)

        for o in ROW_OFFSETS:
            ident = row_id(o)
            d = ident[0] * 2 + ident[1]
            gsend[t, d] = share(d)
            pltpu.make_async_remote_copy(
                src_ref=gsend.at[t, d], dst_ref=grecv.at[t, rho],
                send_sem=ssem.at[5 + t], recv_sem=rsem.at[5 + t],
                device_id=ident, device_id_type=MESH,
            ).start()
        grecv[t, rho] = share(rho)
        if t == 0:
            loglik_over_col(0)
            row = loglik_total(0) * advance
            valid = lax.broadcasted_iota(jnp.int32, (1, TP), 1) < K
            top = jnp.max(jnp.where(valid, row, -jnp.inf))
            clipped = jnp.maximum(row - top, -CLIP_FLOOR)
            norm = jnp.sum(jnp.where(valid, jnp.exp(clipped), 0.0))
            logw = clipped - jnp.log(norm)
            lw_ref[...] = logw[:, :K]
            weight = as_column(jnp.exp(logw))
            acc = jnp.zeros((1, TP), f32)
            for d in range(NR):
                cols = pl.ds(d * WR, WR)
                block = c[:, cols]
                center = jnp.sum(weight * block, axis=0, keepdims=True)
                wide = jnp.sum(weight * (block - center) ** 2, axis=0, keepdims=True) + 1e-06
                spread[:, cols] = wide
                for h in range(WR // TP):
                    acc = acc + wide[:, h * TP:(h + 1) * TP]
            sp_send[0] = acc
            sp_col[me] = acc
            to_col(sp_send.at[0], sp_col.at[me], None, ssem.at[9], rsem.at[9])

        landed(grecv.at[t, pl.ds(0, NR - 1)], rsem.at[5 + t])
        hfull[t, rho] = jnp.sum(grecv[t].astype(f32), axis=0).astype(bf16)
        to_row(hfull.at[t, rho], hfull.at[t, rho], ssem.at[7 + t], rsem.at[7 + t])

        if t == 0:
            landed(sp_col.at[pl.ds(0, NT - 1)], rsem.at[9])
            total = jnp.sum(jnp.sum(sp_col[...], axis=0))
            scale[...] = stepped * (spread[...] / (total / P_SIZE))
        for d in range(NR):
            cols = pl.ds(d * WR, WR)
            now = c[:, cols]
            a = scale[:, cols]
            pull = now / jnp.sqrt(now * now + 1.0)
            moved = now - (SHRINKAGE_LEVEL * a) * pull + jnp.sqrt(2.0 * a) * noise[t, :, cols]
            base[:, cols] = jnp.where(flags[t], moved, now)

        landed(hfull.at[t, pl.ds(0, NR - 1)], rsem.at[7 + t])
        for d in range(NR):
            cols = pl.ds(d * WR, WR)
            gain = jnp.where(flags[t], (upcoming * scale_s) * scale[:, cols], 0.0)
            fresh = base[:, cols] + gain * hfull[t, d].astype(f32)
            c[:, cols] = fresh
            cb[:, cols] = fresh.astype(bf16)
        if t == NMOVE - 1:
            pltpu.make_async_copy(c, out_hbm, osem).start()
        tile = logits_phase(t + 1, ps.at[t], rs.at[t], 1 + t)

    loglik_send(1, tile)
    loglik_over_col(1)
    ml_ref[...] = loglik_total(1)[:, :K] / float(ROWS * NR)

    pltpu.make_async_copy(c, out_hbm, osem).wait()
    landed(pf.at[pl.ds(0, NT - 1)], ssem.at[0])
    for t in range(NMOVE):
        landed(ps.at[t, pl.ds(0, NT - 1)], ssem.at[1 + t])
        landed(resid.at[t, pl.ds(0, NT - 1)], ssem.at[3 + t])
        landed(gsend.at[t, pl.ds(0, NR - 1)], ssem.at[5 + t])
        landed(hfull.at[t, pl.ds(0, NR - 1)], ssem.at[7 + t])
        landed(ll_col.at[t, pl.ds(0, NT - 1)], ssem.at[10 + t])
        landed(llr.at[t, pl.ds(0, NR - 1)], ssem.at[12 + t])
    landed(sp_col.at[pl.ds(0, NT - 1)], ssem.at[9])


def local(doses, status, cloud, noise, flags, heat, advance, drift):
    f32, bf16 = jnp.float32, jnp.bfloat16
    vmem = pl.BlockSpec(memory_space=pltpu.VMEM)
    smem = pl.BlockSpec(memory_space=pltpu.SMEM)
    hbm = pl.BlockSpec(memory_space=pl.ANY)
    particles, logw, mean = pl.pallas_call(
        kernel,
        out_shape=(
            jax.ShapeDtypeStruct((K, COLS), f32),
            jax.ShapeDtypeStruct((1, K), f32),
            jax.ShapeDtypeStruct((1, K), f32),
        ),
        in_specs=[hbm, vmem, hbm, hbm, vmem, smem, smem, smem],
        out_specs=(hbm, vmem, vmem),
        scratch_shapes=[
            pltpu.VMEM((NZ, TP, COLS), jnp.int32),
            pltpu.VMEM((ROWS, COLS), bf16),
            pltpu.VMEM((K, COLS), f32),
            pltpu.VMEM((NMOVE, K, COLS), f32),
            pltpu.VMEM((K, COLS), bf16),
            pltpu.VMEM((K, COLS), f32),
            pltpu.VMEM((1, COLS), f32),
            pltpu.VMEM((1, COLS), f32),
            pltpu.VMEM((K, ROWS), bf16),
            pltpu.VMEM((NT, TK, TP), f32),
            pltpu.VMEM((NT, TK, TP), f32),
            pltpu.VMEM((NMOVE, NT, TK, TP), bf16),
            pltpu.VMEM((NMOVE, NT, TK, TP), bf16),
            pltpu.VMEM((NMOVE, NT, TK, TP), bf16),
            pltpu.VMEM((NMOVE, NR, K, WR), bf16),
            pltpu.VMEM((NMOVE, NR, K, WR), bf16),
            pltpu.VMEM((NMOVE, NR, K, WR), bf16),
            pltpu.VMEM((2, 1, TP), f32),
            pltpu.VMEM((2, NT, 1, TP), f32),
            pltpu.VMEM((2, 1, TP), f32),
            pltpu.VMEM((2, NR, 1, TP), f32),
            pltpu.VMEM((1, 1, TP), f32),
            pltpu.VMEM((NT, 1, TP), f32),
            pltpu.SemaphoreType.DMA((NZ,)),
            pltpu.SemaphoreType.DMA((2,)),
            pltpu.SemaphoreType.DMA,
            pltpu.SemaphoreType.DMA((14,)),
            pltpu.SemaphoreType.DMA((14,)),
        ],
        compiler_params=pltpu.CompilerParams(collective_id=0, has_side_effects=True),
    )(doses, status.reshape(NZ, TP), cloud, noise, jnp.pad(flags, ((0, 0), (0, TP - K))), heat, advance, drift)
    return particles, logw.reshape(K), mean.reshape(K)


def solution(mesh):
    torus = Mesh(mesh.devices.reshape(4, 2, 8, 2, 2), ("row_0", "row_1", "col_0", "col_1", "col_2"))
    return jax.shard_map(
        local,
        mesh=torus,
        in_specs=(P(ROW, COL), P(ROW), P(None, COL), P(None, None, COL), P(), P(), P(), P()),
        out_specs=(P(None, COL), P(), P()),
        check_vma=False,
    )
```

time: 267 us -> 89.5 us (0.34)
  blocking collectives: 154 us -> 0 us
  Pallas kernels: 0 us -> 81.3 us
  waiting for transfers between devices: 47.6 us -> 0 us
  starting transfers between devices: 23.9 us -> 0 us
  other arithmetic: 16.3 us -> 0 us
  matrix products: 9.84 us -> 0 us
  local copies, waits for them, and re-layouts: 9.93 us -> 5.4 us
    pallas_call x0 -> x1, Pallas kernels: none -> 81.3 us  [local(): pl.pallas_call(kernel, out_shape=(jax.ShapeDtypeStruct((K, COLS), f32), j...]
    psum x10 -> x0, blocking collectives: 78.5 us -> none  [one_axis_at_a_time(): shard = lax.psum(shard, axis)]
    all_to_all x4 -> x0, blocking collectives: 75.6 us -> none  [the longest x2 43.7 us: copy_for_each(): return lax.all_to_all(copies, axis, split_axis=0, concat_axis=0, tiled=True)]
    all_to_all x4 -> x0, waiting for transfers between devices: 47.6 us -> none  [the longest x3 36.9 us: copy_for_each(): return lax.all_to_all(copies, axis, split_axis=0, concat_axis=0, tiled=True)]
    all_to_all x4 -> x0, starting transfers between devices: 23.9 us -> none  [the longest x3 12.9 us: copy_for_each(): return lax.all_to_all(copies, axis, split_axis=0, concat_axis=0, tiled=True)]
    dot_general x5 -> x0, matrix products: 9.84 us -> none  [the longest x2 6.12 us: contract_rows(): lax.dot_general(left, right, (((0,), (0,)), ((), ())), preferred_element_...]
    convert_element_type x3 -> x0, other arithmetic: 4.69 us -> none  [the longest x1 4.62 us: local(): centered = (allele_doses - 1).astype(jnp.bfloat16)]
    reduce_sum x12 -> x0, other arithmetic: 3.81 us -> none  [the longest x1 1.22 us: local(): log_weights = clipped - jnp.log(jnp.sum(jnp.exp(clipped)))]
  transfers between devices with their start and end apart: 4 -> 0, of which waited for: 4 -> 0; matrix products, arithmetic and copies ran while one was open for 2% -> 0% of each run, Pallas kernels for 0% -> 0%
where the time goes in v1:
time: 89.5 us; the launch traced here: 89.3 us
  Pallas kernels  81.3 us (91%)
  local copies, waits for them, and re-layouts  5.4 us (6%)
  between operations  2.58 us (3%)
    pallas_call x1, Pallas kernels, local(): pl.pallas_call(kernel, out_shape=(jax.ShapeDtypeStruct((K, COLS), f32), j...  81.3 us
    unnamed x3, local copies, waits for them, and re-layouts  4.16 us

profile of v1, /device:TPU:1, one launch (start us, length us, event | category | flops | bytes accessed | tf_op | source)
XLA Modules:
  0.0 89.3 jit_solution(8757000188698744957)
XLA Ops:
  2.6 1.2 %pad.4.flags_ref = s32[2,128]{1,0:T(2,128)} pad(s32[2,64]{1,0:T(2,128)} %param.12, s32[]{:T(128)} %constant.0.clone.1), padding=0_0x0_64 | pad | bytes 1540 | tf_op jit(solution)/shard_map/jit(_pad)/pad | solution.py:300
  3.8 81.3 %shard_map.103 = (f32[64,2048]{1,0:T(8,128)}, f32[1,64]{1,0:T(1,128)}, f32[1,64]{1,0:T(1,128)}) custom-call(s32[1024,2048]{1,0:T(8,128)} %x_hbm.1, s32[8,128]{1,0:T(8,128)} %bitcast.3, f32[64,2048]{1,0:T(8,128)} %c_hbm.1, f32[2,64,2048]{2,1,0:T(8,128)} %noise_hbm.1, s32[2,128]{1,0:T(2,128)} %pad.4.flags_ref, f32[1]{0:T(128)S(6)} %copy.14.heat_ref, ...), custom_call_target="tpu_custom_call" | custom-call | tf_op jit(solution)/shard_map/pallas_call | solution.py:260
  85.1 1.9 %copy.17 = f32[64,2048]{1,0:T(8,128)} copy(f32[64,2048]{1,0:T(8,128)} %get-tuple-element.12) | data formatting | bytes 1048576
  87.0 1.1 %copy.18 = f32[64]{0:T(128)} copy(f32[64]{0:T(128)} %bitcast.5) | data formatting | bytes 512
  88.1 1.2 %copy.19 = f32[64]{0:T(128)} copy(f32[64]{0:T(128)} %bitcast.4) | data formatting | bytes 512

commit v2 on v1

v2 whole, which is shorter than its diff:
```python
import jax
import jax.numpy as jnp
from jax import lax
from jax.experimental import pallas as pl
from jax.experimental.pallas import tpu as pltpu
from jax.sharding import Mesh
from jax.sharding import PartitionSpec as P

P_SIZE = 65536
K = 64
ROW = ("row_0", "row_1")
COL = ("col_0", "col_1", "col_2")
CLIP_FLOOR = 4.0
SHRINKAGE_LEVEL = 0.5
MESH = pl.DeviceIdType.MESH

ROWS = 1024
COLS = 2048
NZ, NQ, NT, NR = 8, 4, 32, 8
TP = 128
TK = 16
WR = COLS // NR
NMOVE = 2
Z_OFFSETS = (4, 3, 5, 2, 6, 1, 7, 0)
ROW_OFFSETS = ((2, 1), (1, 1), (3, 1), (2, 0), (0, 1), (1, 0), (3, 0))


def kernel(
    x_hbm, y_hbm, c_hbm, noise_hbm, flags_hbm, heat_hbm, adv_hbm, drift_hbm,
    out_hbm, lw_ref, ml_ref,
    xi, xb, c, noise, cb, base, spread, scale, y_ref, flags_ref, heat, adv, drift,
    pp, pq, pf, rf, ps, rs, resid, gsend, grecv, hfull,
    ll_send, ll_col, llr_send, llr, gm_send, gm_got, gm_all,
    xsem, lsem, osem, ssem, rsem, hsem, psem,
):
    f32, bf16 = jnp.float32, jnp.bfloat16
    y, xh = lax.axis_index("row_0"), lax.axis_index("row_1")
    z, xl, co = lax.axis_index("col_0"), lax.axis_index("col_1"), lax.axis_index("col_2")
    q = co * 2 + xl
    me = z * NQ + q
    rho = y * 2 + xh
    scale_s = float(P_SIZE) ** (-0.5)
    zs = [lax.rem(z + o, NZ) for o in Z_OFFSETS]
    peers = [(zd, qd, (y, xh, zd, qd % 2, qd // 2)) for zd in zs[:-1] for qd in range(NQ)]
    for o in range(1, NQ):
        qd = lax.rem(q + o, NQ)
        peers.append((z, qd, (y, xh, z, lax.rem(qd, 2), qd // 2)))
    row_peers = [(lax.rem(y + o[0], 4), lax.rem(xh + o[1], 2), z, xl, co) for o in ROW_OFFSETS]
    row_ids = [p[0] * 2 + p[1] for p in row_peers]
    row_from = [lax.rem(y + 4 - o[0], 4) * 2 + lax.rem(xh + o[1], 2) for o in ROW_OFFSETS]

    def send(src, dst, send_at, recv_at, device):
        pltpu.make_async_remote_copy(
            src_ref=src, dst_ref=dst, send_sem=send_at, recv_sem=recv_at,
            device_id=device, device_id_type=MESH,
        ).start()

    def landed(ref, sem):
        pltpu.make_async_copy(ref, ref, sem).wait()

    def people(zd):
        return pl.ds(pl.multiple_of(zd * TP, TP), TP)

    copy_c = pltpu.make_async_copy(c_hbm, c, lsem.at[0])
    copy_c.start()
    x_copies = [
        pltpu.make_async_copy(x_hbm.at[people(zd)], xi.at[k], xsem.at[k]) for k, zd in enumerate(zs)
    ]

    barrier = pltpu.get_barrier_semaphore()
    for _, _, device in peers:
        pl.semaphore_signal(barrier, inc=1, device_id=device, device_id_type=MESH)
    for device in row_peers:
        pl.semaphore_signal(barrier, inc=1, device_id=device, device_id_type=MESH)

    for copy in x_copies:
        copy.start()
    small = [
        pltpu.make_async_copy(src, dst, lsem.at[1 + i])
        for i, (src, dst) in enumerate((
            (y_hbm, y_ref), (flags_hbm, flags_ref), (heat_hbm, heat), (adv_hbm, adv),
            (drift_hbm, drift), (noise_hbm, noise),
        ))
    ]
    for copy in small:
        copy.start()

    def to_col(src, dst, send_at, recv_at):
        for _, _, device in peers:
            send(src, dst, send_at, recv_at, device)

    def to_row(src, dst, send_at, recv_at):
        for device in row_peers:
            send(src, dst, send_at, recv_at, device)

    def partial(zds):
        block = jnp.concatenate([xb[people(zd), :] for zd in zds], axis=0)
        return lax.dot_general(
            cb[...], block, (((1,), (1,)), ((), ())), preferred_element_type=f32
        )

    def collected(got, n, count):
        landed(got.at[pl.ds(0, count - 1)], rsem.at[n])
        return jnp.sum(got[...].astype(f32), axis=0) * scale_s

    def logits_phase(sent, got, n):
        groups = [(k, k + 1) for k in range(0, NZ, 2)]
        part = partial([zs[k] for k in groups[0]])
        for i, group in enumerate(groups):
            ahead = partial([zs[k] for k in groups[i + 1]]) if i + 1 < len(groups) else None
            for j, k in enumerate(group):
                for qd in range(NQ):
                    block = part[qd * TK:(qd + 1) * TK, j * TP:(j + 1) * TP]
                    sent[zs[k] * NQ + qd] = block.astype(sent.dtype)
                for zd, qd, device in peers[k * NQ:(k + 1) * NQ]:
                    send(sent.at[zd * NQ + qd], got.at[me], ssem.at[n], rsem.at[n], device)
            part = ahead
        got[me] = sent[me]
        return collected(got, n, NT)

    copy_c.wait()
    cb[...] = c[...].astype(bf16)
    half = NZ // 2
    for g in range(2):
        ks = range(g * half, (g + 1) * half)
        for k in ks:
            x_copies[k].wait()
            xb[people(zs[k]), :] = (xi[k].astype(f32) - 1.0).astype(bf16)
        part = partial([zs[k] for k in ks])
        for j, k in enumerate(ks):
            for h in range(2):
                pp[h, k] = part[h * 2 * TK:(h + 1) * 2 * TK, j * TP:(j + 1) * TP]
    pl.semaphore_wait(barrier, NT - 1 + NR - 1)

    other = (y, xh, z, xl, 1 - co)
    for g in range(2):
        ks = pl.ds(g * half, half)
        send(pp.at[1 - co, ks], pq.at[ks], ssem.at[0], psem.at[g], other)
    slot = z * 2 + xl
    for g in range(2):
        landed(pq.at[pl.ds(g * half, half)], psem.at[g])
        for k in range(g * half, (g + 1) * half):
            both = pp[co, k] + pq[k]
            for xd in range(2):
                pf[k, xd] = both[xd * TK:(xd + 1) * TK, :]
            if k < NZ - 1:
                for xd in range(2):
                    send(pf.at[k, xd], rf.at[slot], ssem.at[15], rsem.at[0], (y, xh, zs[k], xd, co))
            else:
                send(pf.at[k, 1 - xl], rf.at[slot], ssem.at[15], rsem.at[0], (y, xh, z, 1 - xl, co))
                rf[slot] = pf[k, xl]

    near = lax.broadcasted_iota(jnp.int32, (K // 2, TP), 1) < K
    gram = jnp.zeros((K, TP), f32)
    for d in range(NR):
        block = c[:, d * WR:(d + 1) * WR]
        block = block - jnp.mean(block, axis=0, keepdims=True)
        gram = gram + lax.dot_general(
            block, jnp.concatenate([block, block], axis=0), (((1,), (1,)), ((), ())),
            precision=lax.Precision.HIGHEST, preferred_element_type=f32,
        )
    folded = jnp.where(near, gram[:K // 2], gram[K // 2:])
    for d in range(NT):
        gm_send[d] = folded[d:d + 1, :]
    for zd, qd, device in peers:
        send(gm_send.at[zd * NQ + qd], gm_got.at[me], ssem.at[9], rsem.at[9], device)
    gm_got[me] = gm_send[me]

    for copy in small:
        copy.wait()
    outcome = y_ref[pl.ds(z, 1), :].astype(f32)
    sub = lax.broadcasted_iota(jnp.int32, (TK, TP), 0)
    lane = lax.broadcasted_iota(jnp.int32, (TK, TP), 1)

    def loglik_row(tile):
        soft = jnp.maximum(tile, 0.0) + jnp.log1p(jnp.exp(-jnp.abs(tile)))
        total = jnp.sum(outcome * tile - soft, axis=1, keepdims=True)
        return jnp.sum(jnp.where(lane == sub + q * TK, total, 0.0), axis=0, keepdims=True)

    eye = lax.broadcasted_iota(jnp.int32, (K, K), 0) == lax.broadcasted_iota(jnp.int32, (K, K), 1)

    def as_column(row):
        return jnp.sum(jnp.where(eye, row, 0.0), axis=1, keepdims=True)

    flags = [as_column(flags_ref[t:t + 1, :].astype(f32)) > 0.5 for t in range(NMOVE)]
    advance = adv[0]
    stepped = drift[0]
    upcoming = heat[0] + advance

    tile = collected(rf, 0, NT // 2)

    def loglik_send(u, tile):
        ll_send[u] = loglik_row(tile)
        ll_col[u, me] = ll_send[u]
        to_col(ll_send.at[u], ll_col.at[u, me], ssem.at[10 + u], rsem.at[10 + u])

    def loglik_over_col(u):
        landed(ll_col.at[u, pl.ds(0, NT - 1)], rsem.at[10 + u])
        llr_send[u] = jnp.sum(ll_col[u], axis=0)
        llr[u, rho] = llr_send[u]
        to_row(llr_send.at[u], llr.at[u, rho], ssem.at[12 + u], rsem.at[12 + u])

    def loglik_total(u):
        landed(llr.at[u, pl.ds(0, NR - 1)], rsem.at[12 + u])
        return jnp.sum(llr[u], axis=0)[:, :K]

    def free_part(t):
        for d in range(NR):
            cols = pl.ds(d * WR, WR)
            now = c[:, cols]
            a = scale[:, cols]
            pull = now / jnp.sqrt(now * now + 1.0)
            moved = now - (SHRINKAGE_LEVEL * a) * pull + jnp.sqrt(2.0 * a) * noise[t, :, cols]
            base[:, cols] = jnp.where(flags[t], moved, now)

    def update(t, d):
        cols = pl.ds(pl.multiple_of(d * WR, WR), WR)
        gain = jnp.where(flags[t], (upcoming * scale_s) * scale[:, cols], 0.0)
        fresh = base[:, cols] + gain * hfull[t, d].astype(f32)
        c[:, cols] = fresh
        cb[:, cols] = fresh.astype(bf16)

    for t in range(NMOVE):
        resid[t, me] = (outcome - jax.nn.sigmoid(tile)).astype(bf16)
        to_col(resid.at[t, me], resid.at[t, me], ssem.at[3 + t], rsem.at[3 + t])
        if t == 0:
            loglik_send(0, tile)
            landed(gm_got.at[pl.ds(0, NT - 1)], rsem.at[9])
            gm_all[me] = jnp.sum(gm_got[...], axis=0)
            to_col(gm_all.at[me], gm_all.at[me], ssem.at[14], rsem.at[14])
        landed(resid.at[t, pl.ds(0, NT - 1)], rsem.at[3 + t])
        if t == 0:
            loglik_over_col(0)

        whole = jnp.concatenate(
            [resid[t, p * NQ:(p + 1) * NQ].reshape(K, TP) for p in range(NZ)], axis=1
        )

        def shares(ds):
            block = jnp.concatenate(
                [xb[:, pl.ds(pl.multiple_of(d * WR, WR), WR)] for d in ds], axis=1
            )
            return jnp.dot(whole, block, preferred_element_type=f32).astype(bf16)

        order = row_ids + [rho]
        grad = shares(order[0:2])
        for g in range(0, NR, 2):
            ahead = shares(order[g + 2:g + 4]) if g + 2 < NR else None
            for j in range(2):
                i = g + j
                block = grad[:, j * WR:(j + 1) * WR]
                if i < NR - 1:
                    gsend[t, order[i]] = block
                    send(gsend.at[t, order[i]], grecv.at[t, rho], ssem.at[5 + t], rsem.at[5 + t], row_peers[i])
                else:
                    grecv[t, rho] = block
            grad = ahead
        if t > 0:
            free_part(t)

        landed(grecv.at[t, pl.ds(0, NR - 1)], rsem.at[5 + t])
        hfull[t, rho] = jnp.sum(grecv[t].astype(f32), axis=0).astype(bf16)
        for i, device in enumerate(row_peers):
            send(hfull.at[t, rho], hfull.at[t, rho], ssem.at[7 + t], hsem.at[t, i], device)

        if t == 0:
            row = loglik_total(0) * advance
            clipped = jnp.maximum(row - jnp.max(row), -CLIP_FLOOR)
            logw = clipped - jnp.log(jnp.sum(jnp.exp(clipped)))
            lw_ref[...] = logw
            weight = as_column(jnp.exp(logw))
            for d in range(NR):
                cols = pl.ds(d * WR, WR)
                block = c[:, cols]
                center = jnp.sum(weight * block, axis=0, keepdims=True)
                spread[:, cols] = jnp.sum(weight * (block - center) ** 2, axis=0, keepdims=True) + 1e-06
            landed(gm_all.at[pl.ds(0, NT - 1)], rsem.at[14])
            wide_sub = lax.broadcasted_iota(jnp.int32, (K, TP), 0)
            wide_lane = lax.rem(lax.broadcasted_iota(jnp.int32, (K, TP), 1), K)
            across = jnp.sum(jnp.where(wide_lane == wide_sub, weight, 0.0), axis=0, keepdims=True)
            term = weight * (jnp.where(wide_lane == wide_sub, 1.0, 0.0) - across)
            term = jnp.where(near, term[:K // 2], term[K // 2:])
            total = jnp.sum(term * gm_all[...].reshape(NT, TP)) + 1e-06 * P_SIZE
            scale[...] = stepped * (spread[...] / (total / P_SIZE))
            free_part(t)
        update(t, rho)
        for i in reversed(range(NR - 1)):
            landed(hfull.at[t, row_from[i]], hsem.at[t, i])
            update(t, row_from[i])
        if t == NMOVE - 1:
            pltpu.make_async_copy(c, out_hbm, osem).start()
        tile = logits_phase(ps.at[t], rs.at[t], 1 + t)

    loglik_send(1, tile)
    loglik_over_col(1)
    ml_ref[...] = loglik_total(1) / float(ROWS * NR)

    pltpu.make_async_copy(c, out_hbm, osem).wait()
    landed(pq, ssem.at[0])
    landed(rf.at[pl.ds(0, NT // 2 - 1)], ssem.at[15])
    for t in range(NMOVE):
        landed(ps.at[t, pl.ds(0, NT - 1)], ssem.at[1 + t])
        landed(resid.at[t, pl.ds(0, NT - 1)], ssem.at[3 + t])
        landed(gsend.at[t, pl.ds(0, NR - 1)], ssem.at[5 + t])
        landed(hfull.at[t, pl.ds(0, NR - 1)], ssem.at[7 + t])
        landed(ll_col.at[t, pl.ds(0, NT - 1)], ssem.at[10 + t])
        landed(llr.at[t, pl.ds(0, NR - 1)], ssem.at[12 + t])
    landed(gm_got.at[pl.ds(0, NT - 1)], ssem.at[9])
    landed(gm_all.at[pl.ds(0, NT - 1)], ssem.at[14])


def finish(c_in, lw_in, ml_in, c_out, lw_out, ml_out, buf, lw, ml, isem, osem):
    count = 4
    rows = K // count
    ins = [pltpu.make_async_copy(c_in.at[pl.ds(i * rows, rows)], buf.at[i], isem.at[i]) for i in range(count)]
    outs = [pltpu.make_async_copy(buf.at[i], c_out.at[pl.ds(i * rows, rows)], osem.at[i]) for i in range(count)]
    for src, via, dst in ((lw_in, lw, lw_out), (ml_in, ml, ml_out)):
        ins.append(pltpu.make_async_copy(src, via, isem.at[len(ins)]))
        outs.append(pltpu.make_async_copy(via, dst, osem.at[len(outs)]))
    for copy in ins:
        copy.start()
    for arrive, leave in zip(ins, outs):
        arrive.wait()
        leave.start()
    for copy in outs:
        copy.wait()


def local(doses, status, cloud, noise, flags, heat, advance, drift):
    f32, bf16 = jnp.float32, jnp.bfloat16
    vmem = pl.BlockSpec(memory_space=pltpu.VMEM)
    hbm = pl.BlockSpec(memory_space=pl.ANY)
    particles, logw, mean = pl.pallas_call(
        kernel,
        out_shape=(
            jax.ShapeDtypeStruct((K, COLS), f32),
            jax.ShapeDtypeStruct((1, K), f32),
            jax.ShapeDtypeStruct((1, K), f32),
        ),
        in_specs=[hbm] * 8,
        out_specs=(hbm, vmem, vmem),
        scratch_shapes=[
            pltpu.VMEM((NZ, TP, COLS), jnp.int32),
            pltpu.VMEM((ROWS, COLS), bf16),
            pltpu.VMEM((K, COLS), f32),
            pltpu.VMEM((NMOVE, K, COLS), f32),
            pltpu.VMEM((K, COLS), bf16),
            pltpu.VMEM((K, COLS), f32),
            pltpu.VMEM((1, COLS), f32),
            pltpu.VMEM((1, COLS), f32),
            pltpu.VMEM((NZ, TP), jnp.int32),
            pltpu.VMEM((NMOVE, K), jnp.int32),
            pltpu.SMEM((1,), f32),
            pltpu.SMEM((1,), f32),
            pltpu.SMEM((1,), f32),
            pltpu.VMEM((2, NZ, 2 * TK, TP), f32),
            pltpu.VMEM((NZ, 2 * TK, TP), f32),
            pltpu.VMEM((NZ, 2, TK, TP), f32),
            pltpu.VMEM((NT // 2, TK, TP), f32),
            pltpu.VMEM((NMOVE, NT, TK, TP), bf16),
            pltpu.VMEM((NMOVE, NT, TK, TP), bf16),
            pltpu.VMEM((NMOVE, NT, TK, TP), bf16),
            pltpu.VMEM((NMOVE, NR, K, WR), bf16),
            pltpu.VMEM((NMOVE, NR, K, WR), bf16),
            pltpu.VMEM((NMOVE, NR, K, WR), bf16),
            pltpu.VMEM((2, 1, TP), f32),
            pltpu.VMEM((2, NT, 1, TP), f32),
            pltpu.VMEM((2, 1, TP), f32),
            pltpu.VMEM((2, NR, 1, TP), f32),
            pltpu.VMEM((NT, 1, TP), f32),
            pltpu.VMEM((NT, 1, TP), f32),
            pltpu.VMEM((NT, 1, TP), f32),
            pltpu.SemaphoreType.DMA((NZ,)),
            pltpu.SemaphoreType.DMA((7,)),
            pltpu.SemaphoreType.DMA,
            pltpu.SemaphoreType.DMA((16,)),
            pltpu.SemaphoreType.DMA((15,)),
            pltpu.SemaphoreType.DMA((NMOVE, NR - 1)),
            pltpu.SemaphoreType.DMA((2,)),
        ],
        compiler_params=pltpu.CompilerParams(collective_id=0, has_side_effects=True),
    )(doses, status.reshape(NZ, TP), cloud, noise, flags, heat, advance, drift)
    particles, logw, mean = pl.pallas_call(
        finish,
        out_shape=(
            jax.ShapeDtypeStruct((K, COLS), f32),
            jax.ShapeDtypeStruct((1, K), f32),
            jax.ShapeDtypeStruct((1, K), f32),
        ),
        in_specs=[hbm] * 3,
        out_specs=(hbm, hbm, hbm),
        scratch_shapes=[
            pltpu.VMEM((4, K // 4, COLS), f32),
            pltpu.VMEM((1, K), f32),
            pltpu.VMEM((1, K), f32),
            pltpu.SemaphoreType.DMA((6,)),
            pltpu.SemaphoreType.DMA((6,)),
        ],
    )(particles, logw, mean)
    return particles, logw.reshape(K), mean.reshape(K)


def solution(mesh):
    torus = Mesh(mesh.devices.reshape(4, 2, 8, 2, 2), ("row_0", "row_1", "col_0", "col_1", "col_2"))
    return jax.shard_map(
        local,
        mesh=torus,
        in_specs=(P(ROW, COL), P(ROW), P(None, COL), P(None, None, COL), P(), P(), P(), P()),
        out_specs=(P(None, COL), P(), P()),
        check_vma=False,
    )
```

time: 89.5 us -> 82.9 us (0.926)
  local copies, waits for them, and re-layouts: 5.4 us -> 0 us
  Pallas kernels: 81.3 us -> 80.2 us
    unnamed x3 -> x0, local copies, waits for them, and re-layouts: 4.16 us -> none
    pallas_call x1, Pallas kernels: 81.3 us -> 78.4 us  [local(): pl.pallas_call(kernel, out_shape=(jax.ShapeDtypeStruct((K, COLS), f32), j...]
    pallas_call x0 -> x1, Pallas kernels: none -> 1.86 us  [local(): pl.pallas_call(finish, out_shape=(jax.ShapeDtypeStruct((K, COLS), f32), j...]
    pad x1 -> x0, local copies, waits for them, and re-layouts: 1.25 us -> none  [local(): jnp.pad(flags, ((0, 0), (0, TP - K)))]
where the time goes in v2:
time: 82.9 us; the launch traced here: 82.8 us
  Pallas kernels  80.2 us (97%)
  between operations  2.58 us (3%)
    pallas_call x1, Pallas kernels, local(): pl.pallas_call(kernel, out_shape=(jax.ShapeDtypeStruct((K, COLS), f32), j...  78.4 us
    pallas_call x1, Pallas kernels, local(): pl.pallas_call(finish, out_shape=(jax.ShapeDtypeStruct((K, COLS), f32), j...  1.86 us

profile of v2, /device:TPU:1, one launch (start us, length us, event | category | flops | bytes accessed | tf_op | source)
XLA Modules:
  0.0 82.8 jit_solution(12132548454261197260)
XLA Ops:
  2.6 78.4 %shard_map.103 = (f32[64,2048]{1,0:T(8,128)}, f32[1,64]{1,0:T(1,128)}, f32[1,64]{1,0:T(1,128)}) custom-call(s32[1024,2048]{1,0:T(8,128)} %x_hbm.1, s32[8,128]{1,0:T(8,128)} %bitcast.3, f32[64,2048]{1,0:T(8,128)} %c_hbm.1, f32[2,64,2048]{2,1,0:T(8,128)} %noise_hbm.1, s32[2,64]{1,0:T(2,128)} %flags_hbm.1, f32[1]{0:T(128)S(6)} %copy.11.heat_hbm, ...), custom_call_target="tpu_custom_call" | custom-call | tf_op jit(solution)/shard_map/pallas_call | solution.py:333
  80.9 1.9 %shard_map.104 = (f32[64,2048]{1,0:T(8,128)}, f32[1,64]{1,0:T(1,128)}, f32[1,64]{1,0:T(1,128)}) custom-call(f32[64,2048]{1,0:T(8,128)} %get-tuple-element.9.c_in, f32[1,64]{1,0:T(1,128)} %get-tuple-element.10.lw_in, f32[1,64]{1,0:T(1,128)} %get-tuple-element.11.ml_in), custom_call_target="tpu_custom_call" | custom-call | tf_op jit(solution)/shard_map/pallas_call | solution.py:383

commit v3 on v2

--- a/solution.py
+++ b/solution.py
@@ -21,17 +21,18 @@
 TK = 16
 WR = COLS // NR
 NMOVE = 2
+AHEAD = 4
 Z_OFFSETS = (4, 3, 5, 2, 6, 1, 7, 0)
 ROW_OFFSETS = ((2, 1), (1, 1), (3, 1), (2, 0), (0, 1), (1, 0), (3, 0))
 
 
 def kernel(
     x_hbm, y_hbm, c_hbm, noise_hbm, flags_hbm, heat_hbm, adv_hbm, drift_hbm,
-    out_hbm, lw_ref, ml_ref,
-    xi, xb, c, noise, cb, base, spread, scale, y_ref, flags_ref, heat, adv, drift,
+    c, lw_ref, ml_ref,
+    xi, xb, noise, cb, base, spread, scale, y_ref, flags_ref, heat, adv, drift,
     pp, pq, pf, rf, ps, rs, resid, gsend, grecv, hfull,
     ll_send, ll_col, llr_send, llr, gm_send, gm_got, gm_all,
-    xsem, lsem, osem, ssem, rsem, hsem, psem,
+    xsem, lsem, ssem, rsem, hsem, psem,
 ):
     f32, bf16 = jnp.float32, jnp.bfloat16
     y, xh = lax.axis_index("row_0"), lax.axis_index("row_1")
@@ -67,14 +68,15 @@
         pltpu.make_async_copy(x_hbm.at[people(zd)], xi.at[k], xsem.at[k]) for k, zd in enumerate(zs)
     ]
 
+    for copy in x_copies[:AHEAD]:
+        copy.start()
+
     barrier = pltpu.get_barrier_semaphore()
     for _, _, device in peers:
         pl.semaphore_signal(barrier, inc=1, device_id=device, device_id_type=MESH)
     for device in row_peers:
         pl.semaphore_signal(barrier, inc=1, device_id=device, device_id_type=MESH)
 
-    for copy in x_copies:
-        copy.start()
     small = [
         pltpu.make_async_copy(src, dst, lsem.at[1 + i])
         for i, (src, dst) in enumerate((
@@ -82,8 +84,6 @@
             (drift_hbm, drift), (noise_hbm, noise),
         ))
     ]
-    for copy in small:
-        copy.start()
 
     def to_col(src, dst, send_at, recv_at):
         for _, _, device in peers:
@@ -118,26 +118,30 @@
         got[me] = sent[me]
         return collected(got, n, NT)
 
-    copy_c.wait()
-    cb[...] = c[...].astype(bf16)
+    def arrive(g):
+        for k in (g, g + 1):
+            x_copies[k].wait()
+            if k + AHEAD < NZ:
+                x_copies[k + AHEAD].start()
+
+    def convert(g):
+        for k in (g, g + 1):
+            xb[people(zs[k]), :] = (xi[k].astype(f32) - 1.0).astype(bf16)
+
+    def keep(g, part):
+        for j in range(2):
+            for h in range(2):
+                pp[h, g + j] = part[h * 2 * TK:(h + 1) * 2 * TK, j * TP:(j + 1) * TP]
+
     half = NZ // 2
-    for g in range(2):
-        ks = range(g * half, (g + 1) * half)
-        for k in ks:
-            x_copies[k].wait()
-            xb[people(zs[k]), :] = (xi[k].astype(f32) - 1.0).astype(bf16)
-        part = partial([zs[k] for k in ks])
-        for j, k in enumerate(ks):
-            for h in range(2):
-                pp[h, k] = part[h * 2 * TK:(h + 1) * 2 * TK, j * TP:(j + 1) * TP]
-    pl.semaphore_wait(barrier, NT - 1 + NR - 1)
-
     other = (y, xh, z, xl, 1 - co)
-    for g in range(2):
+    slot = z * 2 + xl
+
+    def swap(g):
         ks = pl.ds(g * half, half)
         send(pp.at[1 - co, ks], pq.at[ks], ssem.at[0], psem.at[g], other)
-    slot = z * 2 + xl
-    for g in range(2):
+
+    def joined(g):
         landed(pq.at[pl.ds(g * half, half)], psem.at[g])
         for k in range(g * half, (g + 1) * half):
             both = pp[co, k] + pq[k]
@@ -149,6 +153,32 @@
             else:
                 send(pf.at[k, 1 - xl], rf.at[slot], ssem.at[15], rsem.at[0], (y, xh, z, 1 - xl, co))
                 rf[slot] = pf[k, xl]
+
+    arrive(0)
+    convert(0)
+    copy_c.wait()
+    cb[...] = c[...].astype(bf16)
+    part = partial(zs[0:2])
+    arrive(2)
+    convert(2)
+    keep(0, part)
+    part = partial(zs[2:4])
+    arrive(4)
+    convert(4)
+    keep(2, part)
+    pl.semaphore_wait(barrier, NT - 1 + NR - 1)
+    swap(0)
+    part = partial(zs[4:6])
+    arrive(6)
+    convert(6)
+    keep(4, part)
+    joined(0)
+    part = partial(zs[6:8])
+    keep(6, part)
+    swap(1)
+    for copy in small:
+        copy.start()
+    joined(1)
 
     near = lax.broadcasted_iota(jnp.int32, (K // 2, TP), 1) < K
     gram = jnp.zeros((K, TP), f32)
@@ -225,12 +255,7 @@
         to_col(resid.at[t, me], resid.at[t, me], ssem.at[3 + t], rsem.at[3 + t])
         if t == 0:
             loglik_send(0, tile)
-            landed(gm_got.at[pl.ds(0, NT - 1)], rsem.at[9])
-            gm_all[me] = jnp.sum(gm_got[...], axis=0)
-            to_col(gm_all.at[me], gm_all.at[me], ssem.at[14], rsem.at[14])
         landed(resid.at[t, pl.ds(0, NT - 1)], rsem.at[3 + t])
-        if t == 0:
-            loglik_over_col(0)
 
         whole = jnp.concatenate(
             [resid[t, p * NQ:(p + 1) * NQ].reshape(K, TP) for p in range(NZ)], axis=1
@@ -255,7 +280,13 @@
                 else:
                     grecv[t, rho] = block
             grad = ahead
-        if t > 0:
+            if t == 0 and g == 0:
+                loglik_over_col(0)
+        if t == 0:
+            landed(gm_got.at[pl.ds(0, NT - 1)], rsem.at[9])
+            gm_all[me] = jnp.sum(gm_got[...], axis=0)
+            to_col(gm_all.at[me], gm_all.at[me], ssem.at[14], rsem.at[14])
+        else:
             free_part(t)
 
         landed(grecv.at[t, pl.ds(0, NR - 1)], rsem.at[5 + t])
@@ -287,15 +318,12 @@
         for i in reversed(range(NR - 1)):
             landed(hfull.at[t, row_from[i]], hsem.at[t, i])
             update(t, row_from[i])
-        if t == NMOVE - 1:
-            pltpu.make_async_copy(c, out_hbm, osem).start()
         tile = logits_phase(ps.at[t], rs.at[t], 1 + t)
 
     loglik_send(1, tile)
     loglik_over_col(1)
     ml_ref[...] = loglik_total(1) / float(ROWS * NR)
 
-    pltpu.make_async_copy(c, out_hbm, osem).wait()
     landed(pq, ssem.at[0])
     landed(rf.at[pl.ds(0, NT // 2 - 1)], ssem.at[15])
     for t in range(NMOVE):
@@ -309,20 +337,14 @@
     landed(gm_all.at[pl.ds(0, NT - 1)], ssem.at[14])
 
 
-def finish(c_in, lw_in, ml_in, c_out, lw_out, ml_out, buf, lw, ml, isem, osem):
-    count = 4
-    rows = K // count
-    ins = [pltpu.make_async_copy(c_in.at[pl.ds(i * rows, rows)], buf.at[i], isem.at[i]) for i in range(count)]
-    outs = [pltpu.make_async_copy(buf.at[i], c_out.at[pl.ds(i * rows, rows)], osem.at[i]) for i in range(count)]
-    for src, via, dst in ((lw_in, lw, lw_out), (ml_in, ml, ml_out)):
-        ins.append(pltpu.make_async_copy(src, via, isem.at[len(ins)]))
-        outs.append(pltpu.make_async_copy(via, dst, osem.at[len(outs)]))
-    for copy in ins:
+def finish(c_in, lw_in, ml_in, c_out, lw_out, ml_out, sem):
+    copies = [
+        pltpu.make_async_copy(src, dst, sem.at[i])
+        for i, (src, dst) in enumerate(((ml_in, ml_out), (lw_in, lw_out), (c_in, c_out)))
+    ]
+    for copy in copies:
         copy.start()
-    for arrive, leave in zip(ins, outs):
-        arrive.wait()
-        leave.start()
-    for copy in outs:
+    for copy in copies:
         copy.wait()
 
 
@@ -333,16 +355,15 @@
     particles, logw, mean = pl.pallas_call(
         kernel,
         out_shape=(
-            jax.ShapeDtypeStruct((K, COLS), f32),
-            jax.ShapeDtypeStruct((1, K), f32),
-            jax.ShapeDtypeStruct((1, K), f32),
+            pltpu.VMEM((K, COLS), f32),
+            pltpu.VMEM((1, K), f32),
+            pltpu.VMEM((1, K), f32),
         ),
         in_specs=[hbm] * 8,
-        out_specs=(hbm, vmem, vmem),
+        out_specs=(vmem, vmem, vmem),
         scratch_shapes=[
             pltpu.VMEM((NZ, TP, COLS), jnp.int32),
             pltpu.VMEM((ROWS, COLS), bf16),
-            pltpu.VMEM((K, COLS), f32),
             pltpu.VMEM((NMOVE, K, COLS), f32),
             pltpu.VMEM((K, COLS), bf16),
             pltpu.VMEM((K, COLS), f32),
@@ -372,7 +393,6 @@
             pltpu.VMEM((NT, 1, TP), f32),
             pltpu.SemaphoreType.DMA((NZ,)),
             pltpu.SemaphoreType.DMA((7,)),
-            pltpu.SemaphoreType.DMA,
             pltpu.SemaphoreType.DMA((16,)),
             pltpu.SemaphoreType.DMA((15,)),
             pltpu.SemaphoreType.DMA((NMOVE, NR - 1)),
@@ -387,15 +407,10 @@
             jax.ShapeDtypeStruct((1, K), f32),
             jax.ShapeDtypeStruct((1, K), f32),
         ),
-        in_specs=[hbm] * 3,
+        in_specs=[vmem] * 3,
         out_specs=(hbm, hbm, hbm),
-        scratch_shapes=[
-            pltpu.VMEM((4, K // 4, COLS), f32),
-            pltpu.VMEM((1, K), f32),
-            pltpu.VMEM((1, K), f32),
-            pltpu.SemaphoreType.DMA((6,)),
-            pltpu.SemaphoreType.DMA((6,)),
-        ],
+        scratch_shapes=[pltpu.SemaphoreType.DMA((3,))],
+        compiler_params=pltpu.CompilerParams(vmem_limit_bytes=1 << 20),
     )(particles, logw, mean)
     return particles, logw.reshape(K), mean.reshape(K)
 

time: 82.9 us -> 79.2 us (0.955)
  Pallas kernels: 80.2 us -> 76.5 us
    pallas_call x1, Pallas kernels: 78.4 us -> 75.7 us  [local(): pl.pallas_call(kernel, out_shape=(pltpu.VMEM((K, COLS), f32), pltpu.VMEM(...]
    pallas_call x1, Pallas kernels: 1.86 us -> 0.83 us  [local(): pl.pallas_call(finish, out_shape=(jax.ShapeDtypeStruct((K, COLS), f32), j...]
where the time goes in v3:
time: 79.2 us; the launch traced here: 79.1 us
  Pallas kernels  76.5 us (97%)
  between operations  2.58 us (3%)
    pallas_call x1, Pallas kernels, local(): pl.pallas_call(kernel, out_shape=(pltpu.VMEM((K, COLS), f32), pltpu.VMEM(...  75.7 us

profile of v3, /device:TPU:1, one launch (start us, length us, event | category | flops | bytes accessed | tf_op | source)
XLA Modules:
  0.0 79.1 jit_solution(6362822727942750114)
XLA Ops:
  2.6 75.7 %shard_map.103 = (f32[64,2048]{1,0:T(8,128)S(1)}, f32[1,64]{1,0:T(1,128)S(1)}, f32[1,64]{1,0:T(1,128)S(1)}) custom-call(s32[1024,2048]{1,0:T(8,128)} %x_hbm.1, s32[8,128]{1,0:T(8,128)} %bitcast.3, f32[64,2048]{1,0:T(8,128)} %c_hbm.1, f32[2,64,2048]{2,1,0:T(8,128)} %noise_hbm.1, s32[2,64]{1,0:T(2,128)} %flags_hbm.1, f32[1]{0:T(128)S(6)} %copy.11.heat_hbm, ...), custom_call_target="tpu_custom_call" | custom-call | tf_op jit(solution)/shard_map/pallas_call | solution.py:355
  78.3 0.8 %shard_map.104 = (f32[64,2048]{1,0:T(8,128)}, f32[1,64]{1,0:T(1,128)}, f32[1,64]{1,0:T(1,128)}) custom-call(f32[64,2048]{1,0:T(8,128)S(1)} %get-tuple-element.9.c_in, f32[1,64]{1,0:T(1,128)S(1)} %get-tuple-element.10.lw_in, f32[1,64]{1,0:T(1,128)S(1)} %get-tuple-element.11.ml_in), custom_call_target="tpu_custom_call" | custom-call | tf_op jit(solution)/shard_map/pallas_call | solution.py:403

commit v4 on v3

--- a/solution.py
+++ b/solution.py
@@ -21,6 +21,11 @@
 TK = 16
 WR = COLS // NR
 NMOVE = 2
+NALL = 128
+ALL_OFFSETS = sorted(
+    ((a, b, c, d) for a in range(4) for b in range(2) for c in range(8) for d in range(2) if a + b + c + d),
+    key=lambda o: -(min(o[0], 4 - o[0]) + min(o[2], 8 - o[2]) + (0, 1, 2, 1)[2 * o[1] + o[3]]),
+)
 AHEAD = 4
 Z_OFFSETS = (4, 3, 5, 2, 6, 1, 7, 0)
 ROW_OFFSETS = ((2, 1), (1, 1), (3, 1), (2, 0), (0, 1), (1, 0), (3, 0))
@@ -31,7 +36,7 @@
     c, lw_ref, ml_ref,
     xi, xb, noise, cb, base, spread, scale, y_ref, flags_ref, heat, adv, drift,
     pp, pq, pf, rf, ps, rs, resid, gsend, grecv, hfull,
-    ll_send, ll_col, llr_send, llr, gm_send, gm_got, gm_all,
+    fin_pair, fin_send, fin_all, ll_send, ll_col, llr_send, llr, gm_send, gm_got, gm_all,
     xsem, lsem, ssem, rsem, hsem, psem,
 ):
     f32, bf16 = jnp.float32, jnp.bfloat16
@@ -320,9 +325,20 @@
             update(t, row_from[i])
         tile = logits_phase(ps.at[t], rs.at[t], 1 + t)
 
-    loglik_send(1, tile)
-    loglik_over_col(1)
-    ml_ref[...] = loglik_total(1) / float(ROWS * NR)
+    fin_pair[0] = loglik_row(tile)
+    send(fin_pair.at[0], fin_pair.at[1], ssem.at[11], rsem.at[11], other)
+    landed(fin_pair.at[1], rsem.at[11])
+    fin_send[0] = fin_pair[0] + fin_pair[1]
+    mine = (rho * NZ + z) * 2 + xl
+    fin_all[mine] = fin_send[0]
+    ys = [lax.rem(y + o, 4) for o in range(4)]
+    xhs = [lax.rem(xh + o, 2) for o in range(2)]
+    zz = [lax.rem(z + o, NZ) for o in range(NZ)]
+    xls = [lax.rem(xl + o, 2) for o in range(2)]
+    for dy, dx, dz, dl in ALL_OFFSETS:
+        send(fin_send.at[0], fin_all.at[mine], ssem.at[13], rsem.at[13], (ys[dy], xhs[dx], zz[dz], xls[dl], co))
+    landed(fin_all.at[pl.ds(0, NALL - 1)], rsem.at[13])
+    ml_ref[...] = jnp.sum(fin_all[...], axis=0)[:, :K] / float(ROWS * NR)
 
     landed(pq, ssem.at[0])
     landed(rf.at[pl.ds(0, NT // 2 - 1)], ssem.at[15])
@@ -331,8 +347,10 @@
         landed(resid.at[t, pl.ds(0, NT - 1)], ssem.at[3 + t])
         landed(gsend.at[t, pl.ds(0, NR - 1)], ssem.at[5 + t])
         landed(hfull.at[t, pl.ds(0, NR - 1)], ssem.at[7 + t])
-        landed(ll_col.at[t, pl.ds(0, NT - 1)], ssem.at[10 + t])
-        landed(llr.at[t, pl.ds(0, NR - 1)], ssem.at[12 + t])
+    landed(ll_col.at[0, pl.ds(0, NT - 1)], ssem.at[10])
+    landed(llr.at[0, pl.ds(0, NR - 1)], ssem.at[12])
+    landed(fin_pair.at[1], ssem.at[11])
+    landed(fin_all.at[pl.ds(0, NALL - 1)], ssem.at[13])
     landed(gm_got.at[pl.ds(0, NT - 1)], ssem.at[9])
     landed(gm_all.at[pl.ds(0, NT - 1)], ssem.at[14])
 
@@ -385,9 +403,12 @@
             pltpu.VMEM((NMOVE, NR, K, WR), bf16),
             pltpu.VMEM((NMOVE, NR, K, WR), bf16),
             pltpu.VMEM((2, 1, TP), f32),
-            pltpu.VMEM((2, NT, 1, TP), f32),
-            pltpu.VMEM((2, 1, TP), f32),
-            pltpu.VMEM((2, NR, 1, TP), f32),
+            pltpu.VMEM((1, 1, TP), f32),
+            pltpu.VMEM((NALL, 1, TP), f32),
+            pltpu.VMEM((1, 1, TP), f32),
+            pltpu.VMEM((1, NT, 1, TP), f32),
+            pltpu.VMEM((1, 1, TP), f32),
+            pltpu.VMEM((1, NR, 1, TP), f32),
             pltpu.VMEM((NT, 1, TP), f32),
             pltpu.VMEM((NT, 1, TP), f32),
             pltpu.VMEM((NT, 1, TP), f32),

time: 79.2 us -> 78.5 us (level)
  no operation moved by 1% of the time
where the time goes in v4:
time: 78.5 us; the launch traced here: 78.4 us
  Pallas kernels  75.8 us (97%)
  between operations  2.58 us (3%)
    pallas_call x1, Pallas kernels, local(): pl.pallas_call(kernel, out_shape=(pltpu.VMEM((K, COLS), f32), pltpu.VMEM(...  75 us

profile of v4, /device:TPU:1, one launch (start us, length us, event | category | flops | bytes accessed | tf_op | source)
XLA Modules:
  0.0 78.4 jit_solution(11733919256671445607)
XLA Ops:
  2.6 75.0 %shard_map.103 = (f32[64,2048]{1,0:T(8,128)S(1)}, f32[1,64]{1,0:T(1,128)S(1)}, f32[1,64]{1,0:T(1,128)S(1)}) custom-call(s32[1024,2048]{1,0:T(8,128)} %x_hbm.1, s32[8,128]{1,0:T(8,128)} %bitcast.3, f32[64,2048]{1,0:T(8,128)} %c_hbm.1, f32[2,64,2048]{2,1,0:T(8,128)} %noise_hbm.1, s32[2,64]{1,0:T(2,128)} %flags_hbm.1, f32[1]{0:T(128)S(6)} %copy.11.heat_hbm, ...), custom_call_target="tpu_custom_call" | custom-call | tf_op jit(solution)/shard_map/pallas_call | solution.py:373
  77.5 0.8 %shard_map.104 = (f32[64,2048]{1,0:T(8,128)}, f32[1,64]{1,0:T(1,128)}, f32[1,64]{1,0:T(1,128)}) custom-call(f32[64,2048]{1,0:T(8,128)S(1)} %get-tuple-element.9.c_in, f32[1,64]{1,0:T(1,128)S(1)} %get-tuple-element.10.lw_in, f32[1,64]{1,0:T(1,128)S(1)} %get-tuple-element.11.ml_in), custom_call_target="tpu_custom_call" | custom-call | tf_op jit(solution)/shard_map/pallas_call | solution.py:424

commit v5 on v4

--- a/solution.py
+++ b/solution.py
@@ -112,14 +112,14 @@
         groups = [(k, k + 1) for k in range(0, NZ, 2)]
         part = partial([zs[k] for k in groups[0]])
         for i, group in enumerate(groups):
-            ahead = partial([zs[k] for k in groups[i + 1]]) if i + 1 < len(groups) else None
+            ahead = partial([zs[k] for k in groups[i + 1]]) if 0 < i < len(groups) - 1 else None
             for j, k in enumerate(group):
                 for qd in range(NQ):
                     block = part[qd * TK:(qd + 1) * TK, j * TP:(j + 1) * TP]
                     sent[zs[k] * NQ + qd] = block.astype(sent.dtype)
                 for zd, qd, device in peers[k * NQ:(k + 1) * NQ]:
                     send(sent.at[zd * NQ + qd], got.at[me], ssem.at[n], rsem.at[n], device)
-            part = ahead
+            part = partial([zs[k] for k in groups[1]]) if i == 0 else ahead
         got[me] = sent[me]
         return collected(got, n, NT)
 
@@ -275,7 +275,7 @@
         order = row_ids + [rho]
         grad = shares(order[0:2])
         for g in range(0, NR, 2):
-            ahead = shares(order[g + 2:g + 4]) if g + 2 < NR else None
+            ahead = shares(order[g + 2:g + 4]) if 0 < g < NR - 2 else None
             for j in range(2):
                 i = g + j
                 block = grad[:, j * WR:(j + 1) * WR]
@@ -284,7 +284,7 @@
                     send(gsend.at[t, order[i]], grecv.at[t, rho], ssem.at[5 + t], rsem.at[5 + t], row_peers[i])
                 else:
                     grecv[t, rho] = block
-            grad = ahead
+            grad = shares(order[2:4]) if g == 0 else ahead
             if t == 0 and g == 0:
                 loglik_over_col(0)
         if t == 0:

time: 78.5 us -> 78.7 us (level)
  no operation moved by 1% of the time
where the time goes in v5:
time: 78.7 us; the launch traced here: 78.6 us
  Pallas kernels  76 us (97%)
  between operations  2.58 us (3%)
    pallas_call x1, Pallas kernels, local(): pl.pallas_call(kernel, out_shape=(pltpu.VMEM((K, COLS), f32), pltpu.VMEM(...  75.2 us

profile of v5, /device:TPU:1, one launch (start us, length us, event | category | flops | bytes accessed | tf_op | source)
XLA Modules:
  0.0 78.6 jit_solution(2289151239357432275)
XLA Ops:
  2.6 75.2 %shard_map.103 = (f32[64,2048]{1,0:T(8,128)S(1)}, f32[1,64]{1,0:T(1,128)S(1)}, f32[1,64]{1,0:T(1,128)S(1)}) custom-call(s32[1024,2048]{1,0:T(8,128)} %x_hbm.1, s32[8,128]{1,0:T(8,128)} %bitcast.3, f32[64,2048]{1,0:T(8,128)} %c_hbm.1, f32[2,64,2048]{2,1,0:T(8,128)} %noise_hbm.1, s32[2,64]{1,0:T(2,128)} %flags_hbm.1, f32[1]{0:T(128)S(6)} %copy.11.heat_hbm, ...), custom_call_target="tpu_custom_call" | custom-call | tf_op jit(solution)/shard_map/pallas_call | solution.py:373
  77.8 0.8 %shard_map.104 = (f32[64,2048]{1,0:T(8,128)}, f32[1,64]{1,0:T(1,128)}, f32[1,64]{1,0:T(1,128)}) custom-call(f32[64,2048]{1,0:T(8,128)S(1)} %get-tuple-element.9.c_in, f32[1,64]{1,0:T(1,128)S(1)} %get-tuple-element.10.lw_in, f32[1,64]{1,0:T(1,128)S(1)} %get-tuple-element.11.ml_in), custom_call_target="tpu_custom_call" | custom-call | tf_op jit(solution)/shard_map/pallas_call | solution.py:424
